TPU v7x, 32 devices: a whole 2x2x4 slice. The times are simulated.
32 devices in a mesh: step: 8 (over y, x, core), rows: 4 (over z).
Axes of the slice: x: 2, y: 2, z: 4, core: 2. Of those that a mesh axis runs over, the one named last changes fastest.
Arguments:
- init_states: float32 [8, 1, 2, 77, 384], P('step', None, None, None, 'rows'), may hold values from -63 to 63
- forcing: float32 [8, 1, 4, 384], P('step', None, None, 'rows'), may hold values from -63 to 63
- history: int32 [8, 1], P('step'), may hold values from 1 to 2
- land_mask: int32 [384], P('rows'), may hold values 0 or 1
- w_in: float32 [800, 158], replicated, may hold values from -0.5 to 0.5
- b_in: float32 [800], replicated, may hold values from -1.5 to 1.5
- w_dw: float32 [800, 7, 7], replicated, may hold values from -0.875 to 0.875
- bn_gain: float32 [800], replicated, may hold values from 0.5 to 1.5
- bn_bias: float32 [800], replicated, may hold values from -1.5 to 1.5
- w_up: float32 [3200, 800], replicated, may hold values from -0.21875 to 0.21875
- b_up: float32 [3200], replicated, may hold values from -1.5 to 1.5
- w_down: float32 [800, 3200], replicated, may hold values from -0.109375 to 0.109375
- b_down: float32 [800], replicated, may hold values from -1.5 to 1.5
- w_out: float32 [77, 800], replicated, may hold values from -0.21875 to 0.21875
- b_out: float32 [77], replicated, may hold values from -1.5 to 1.5
- cotangent: float32 [8, 8, 1, 77, 384], P('step', None, None, None, 'rows'), may hold values from -6 to 6
Outputs:
- predicted: float32 [8, 8, 1, 77, 384], P('step', None, None, None, 'rows')
- grad_init: float32 [8, 1, 2, 77, 384], P('step', None, None, None, 'rows')
- grad_forcing: float32 [8, 1, 4, 384], P('step', None, None, 'rows')
- grad_w_in: float32 [800, 158], replicated
- grad_b_in: float32 [800], replicated
- grad_w_dw: float32 [800, 7, 7], replicated
- grad_bn_gain: float32 [800], replicated
- grad_bn_bias: float32 [800], replicated
- grad_w_up: float32 [3200, 800], P('step', 'rows')
- grad_b_up: float32 [3200], replicated
- grad_w_down: float32 [800, 3200], P('rows', 'step')
- grad_b_down: float32 [800], replicated
- grad_w_out: float32 [77, 800], replicated
- grad_b_out: float32 [77], replicated
All inputs are finite; a program needn't handle non-finite values. No bound on the sum of `land_mask` on one device may be relied on, other than what follows from the above.
Results may differ from a plain program's by a relative error of at most 0.0003.
Values sent between devices are 32-bit elements; how exact they have to be, the bound alone decides.
No kernel may reach another device: no remote copies, remote signals or barrier semaphores. Data moves between devices by JAX's collectives and lax.ppermute only.
A program may use at most 448 MiB of HBM per device.

v0:
```python
import jax
import jax.numpy as jnp
from jax import lax
from jax.sharding import PartitionSpec as P

HALO = 3
ROLL = 8
COLS = 32
EPSILON = 1e-05
HIGHEST = lax.Precision.HIGHEST


def padded(cells, sides, width):
    for axis, dim in sides:
        count = lax.axis_size(axis)
        ends = count - 1
        head = lax.slice_in_dim(cells, 0, width, axis=dim)
        tail = lax.slice_in_dim(cells, cells.shape[dim] - width, cells.shape[dim], axis=dim)
        cells = jnp.concatenate(
            [
                lax.ppermute(tail, axis, [(i, (i + 1) % count) for i in range(ends)]),
                cells,
                lax.ppermute(head, axis, [((i + 1) % count, i) for i in range(ends)]),
            ],
            axis=dim,
        )
    return cells


def passed_along(x, axis, by):
    devices = lax.axis_size(axis)
    return lax.ppermute(x, axis, [(i, (i + by) % devices) for i in range(devices)])


def gelu_exact(values):
    return jax.nn.gelu(values, approximate=False)


def depthwise(extended, kernel):
    kernel_width = kernel.shape[-1]
    reach_rows = kernel_width // 2
    rows_out = extended.shape[-1] // COLS - 2 * reach_rows
    column = jnp.arange(extended.shape[-1]) % COLS
    accumulated = jnp.zeros(extended.shape[:-1] + (rows_out * COLS,), jnp.float32)
    for tap_col in range(kernel_width):
        offset = tap_col - reach_rows
        shifted = jnp.roll(extended, -offset, axis=-1)
        inside = (column + offset >= 0) & (column + offset < COLS)
        shifted = jnp.where(inside, shifted, jnp.zeros_like(shifted))
        for tap_row in range(kernel_width):
            piece = shifted[..., tap_row * COLS : (tap_row + rows_out) * COLS]
            accumulated = accumulated + kernel[:, tap_row, tap_col, None] * piece
    return accumulated


def contract(weights, values):
    return jnp.einsum("dc,bcp->bdp", weights, values, precision=HIGHEST)


def transposed(weights, values):
    return jnp.einsum("dc,bdp->bcp", weights, values, precision=HIGHEST)


def outer_sum(first_factor, second_factor):
    return jnp.einsum("bdp,bcp->dc", first_factor, second_factor, precision=HIGHEST)


def reduce_forces(grad_forces):
    accumulated = grad_forces[0]
    for grad_force in grad_forces[1:]:
        accumulated = accumulated + grad_force
    return accumulated


def per_device(
    init_states,
    forcing,
    history,
    land_mask,
    w_in,
    b_in,
    w_dw,
    bn_gain,
    bn_bias,
    w_up,
    b_up,
    w_down,
    b_down,
    w_out,
    b_out,
    cotangent,
):
    ocean_mask = land_mask.astype(jnp.float32)
    local_count = jnp.sum(ocean_mask)
    states = w_out.shape[0]
    rim_cells = HALO * COLS

    def backward_tick(grad_new, kept_tick, grad_list):
        inputs_all, lifted_ext, normalized, inverse_std, ocean_count, residual = kept_tick
        (
            grad_w_in,
            grad_b_in,
            grad_w_dw,
            grad_bn_gain,
            grad_bn_bias,
            grad_w_up,
            grad_b_up,
            grad_w_down,
            grad_b_down,
            grad_w_out,
            grad_b_out,
        ) = grad_list
        grad_masked = grad_new * ocean_mask
        grad_b_out = grad_b_out + jnp.sum(grad_masked, axis=(0, 2))
        grad_w_out = grad_w_out + outer_sum(grad_masked, residual)
        grad_branch = transposed(w_out, grad_masked) * ocean_mask
        normed = normalized * bn_gain[:, None] + bn_bias[:, None]
        hidden_pre = contract(w_up, normed) + b_up[:, None]
        activated, gelu_back = jax.vjp(gelu_exact, hidden_pre)
        grad_b_down = grad_b_down + jnp.sum(grad_branch, axis=(0, 2))
        grad_w_down = grad_w_down + outer_sum(grad_branch, activated)
        grad_hidden = gelu_back(transposed(w_down, grad_branch))[0]
        grad_b_up = grad_b_up + jnp.sum(grad_hidden, axis=(0, 2))
        grad_w_up = grad_w_up + outer_sum(grad_hidden, normed)
        grad_normed = transposed(w_up, grad_hidden)
        local_bias = jnp.sum(grad_normed, axis=-1)
        local_gain = jnp.sum(grad_normed * normalized, axis=-1)
        grad_bn_bias = grad_bn_bias + jnp.sum(local_bias, axis=0)
        grad_bn_gain = grad_bn_gain + jnp.sum(local_gain, axis=0)
        total_bias, total_gain = lax.psum((local_bias, local_gain), "rows")
        correction = (
            ocean_mask * (total_bias[..., None] + normalized * total_gain[..., None]) / ocean_count
        )
        grad_mixed = inverse_std[..., None] * bn_gain[:, None] * (grad_normed - correction)
        grad_ext = padded(grad_mixed, (("rows", 2),), rim_cells)
        grad_lifted = depthwise(grad_ext, w_dw[:, ::-1, ::-1]) + grad_branch
        unused_out, kernel_back = jax.vjp(lambda kernel: depthwise(lifted_ext, kernel), w_dw)
        grad_w_dw = grad_w_dw + kernel_back(grad_mixed)[0]
        grad_b_in = grad_b_in + jnp.sum(grad_lifted, axis=(0, 2))
        grad_w_in = grad_w_in + outer_sum(grad_lifted, inputs_all)
        grad_inputs = transposed(w_in, grad_lifted)
        grad_list = (
            grad_w_in,
            grad_b_in,
            grad_w_dw,
            grad_bn_gain,
            grad_bn_bias,
            grad_w_up,
            grad_b_up,
            grad_w_down,
            grad_b_down,
            grad_w_out,
            grad_b_out,
        )
        return (
            grad_inputs[:, :states],
            grad_inputs[:, states : 2 * states],
            grad_inputs[:, 2 * states :],
            grad_list,
        )

    forcings = [forcing[0] for rollout_step in range(ROLL)]
    cotangents = [cotangent[0, rollout_step] for rollout_step in range(ROLL)]
    current = init_states[0, :, 1]
    previous = jnp.where(
        (history[0] == 2)[:, None, None], init_states[0, :, 0], init_states[0, :, 1]
    )
    outputs = []
    kept_all = []
    for rollout_step in range(ROLL):
        if rollout_step > 0:
            current, previous = passed_along((outputs[-1], current), "step", 1)
        inputs_all = jnp.concatenate([previous, current, forcings[rollout_step]], axis=1)
        lifted = contract(w_in, inputs_all) + b_in[:, None]
        forward_lifted_ext = padded(lifted, (("rows", 2),), rim_cells)
        mixed_cells = depthwise(forward_lifted_ext, w_dw)
        first_sum = jnp.sum(mixed_cells * ocean_mask, axis=-1)
        second_sum = jnp.sum(mixed_cells * mixed_cells * ocean_mask, axis=-1)
        first_total, second_total, forward_ocean_count = lax.psum(
            (first_sum, second_sum, local_count), "rows"
        )
        forward_ocean_count = jnp.maximum(forward_ocean_count, 1.0)
        average = first_total / forward_ocean_count
        variance = second_total / forward_ocean_count - average * average
        forward_inverse_std = lax.rsqrt(variance + EPSILON)
        forward_normalized = (mixed_cells - average[..., None]) * forward_inverse_std[..., None]
        forward_normed = forward_normalized * bn_gain[:, None] + bn_bias[:, None]
        forward_hidden_pre = contract(w_up, forward_normed) + b_up[:, None]
        branch = contract(w_down, gelu_exact(forward_hidden_pre)) + b_down[:, None]
        forward_residual = (lifted + branch) * ocean_mask
        new_state = (contract(w_out, forward_residual) + b_out[:, None]) * ocean_mask
        new_state, kept_tick = (
            new_state,
            (
                inputs_all,
                forward_lifted_ext,
                forward_normalized,
                forward_inverse_std,
                forward_ocean_count,
                forward_residual,
            ),
        )
        outputs.append(new_state)
        kept_all.append(kept_tick)
    grad_list = (
        jnp.zeros_like(w_in),
        jnp.zeros_like(b_in),
        jnp.zeros_like(w_dw),
        jnp.zeros_like(bn_gain),
        jnp.zeros_like(bn_bias),
        jnp.zeros_like(w_up),
        jnp.zeros_like(b_up),
        jnp.zeros_like(w_down),
        jnp.zeros_like(b_down),
        jnp.zeros_like(w_out),
        jnp.zeros_like(b_out),
    )
    grad_forces = [None] * ROLL
    sent_cur = None
    sent_prev = None
    for rollout_step in reversed(range(ROLL)):
        grad_new = cotangents[rollout_step]
        if rollout_step < ROLL - 1:
            came_cur, came_prev = passed_along((sent_cur, sent_prev), "step", -1)
            grad_new = grad_new + came_cur
        grad_prev, grad_cur, grad_force, grad_list = backward_tick(
            grad_new, kept_all[rollout_step], grad_list
        )
        if rollout_step < ROLL - 1:
            grad_cur = grad_cur + came_prev
        sent_cur, sent_prev = (grad_cur, grad_prev)
        grad_forces[rollout_step] = grad_force
    single_history = (history[0] == 1)[:, None, None]
    double_history = (history[0] == 2)[:, None, None]
    grad_init_cur = sent_cur + jnp.where(single_history, sent_prev, jnp.zeros_like(sent_prev))
    grad_init_prev = jnp.where(double_history, sent_prev, jnp.zeros_like(sent_prev))
    grad_init = jnp.stack([grad_init_prev, grad_init_cur], axis=1)[None]
    predicted = jnp.stack(outputs, axis=0)[None]
    grad_forcing = reduce_forces(grad_forces)[None]
    (
        grad_w_in,
        grad_b_in,
        grad_w_dw,
        grad_bn_gain,
        grad_bn_bias,
        grad_w_up,
        grad_b_up,
        grad_w_down,
        grad_b_down,
        grad_w_out,
        grad_b_out,
    ) = grad_list
    small_totals = lax.psum(
        (
            grad_w_in,
            grad_b_in,
            grad_w_dw,
            grad_bn_gain,
            grad_bn_bias,
            grad_b_up,
            grad_b_down,
            grad_w_out,
            grad_b_out,
        ),
        ("step", "rows"),
    )
    shares = (
        lax.psum_scatter(grad_w_up, "step", scatter_dimension=0, tiled=True),
        lax.psum_scatter(grad_w_down, "step", scatter_dimension=1, tiled=True),
    )
    share_up, share_down = (
        lax.psum_scatter(shares[0], "rows", scatter_dimension=1, tiled=True),
        lax.psum_scatter(shares[1], "rows", scatter_dimension=0, tiled=True),
    )
    return (
        predicted,
        grad_init,
        grad_forcing,
        small_totals[0],
        small_totals[1],
        small_totals[2],
        small_totals[3],
        small_totals[4],
        share_up,
        small_totals[5],
        share_down,
        small_totals[6],
        small_totals[7],
        small_totals[8],
    )


def solution(mesh):
    in_specs = (
        P("step", None, None, None, "rows"),
        P("step", None, None, "rows"),
        P("step", None),
        P("rows"),
        P(),
        P(),
        P(),
        P(),
        P(),
        P(),
        P(),
        P(),
        P(),
        P(),
        P(),
        P("step", None, None, None, "rows"),
    )
    out_specs = (
        P("step", None, None, None, "rows"),
        P("step", None, None, None, "rows"),
        P("step", None, None, "rows"),
        P(),
        P(),
        P(),
        P(),
        P(),
        P("step", "rows"),
        P(),
        P("rows", "step"),
        P(),
        P(),
        P(),
    )
    return jax.shard_map(
        per_device, mesh=mesh, in_specs=in_specs, out_specs=out_specs, check_vma=False
    )
```

profile of v0, /device:TPU:0, one launch (start us, length us, event | category | flops | bytes accessed | tf_op | source)
XLA Modules:
  0.0 1748.8 jit_solution(15639221785140882595)
XLA Ops:
  58.7 16.4 fusion.392
  123.4 16.4 fusion.377
  188.8 16.4 fusion.362
  253.5 16.4 fusion.347
  317.9 16.4 fusion.332
  382.8 16.4 fusion.317
  448.6 16.4 fusion.302
  516.0 12.9 fusion.1177
  589.5 11.1 fusion.848
  757.7 13.4 fusion.43
  808.4 12.9 fusion.39
  833.9 13.5 fusion.35
  869.6 11.2 all-reduce.396
  885.3 12.9 fusion.31
  910.2 13.5 fusion.27
  945.8 11.5 all-reduce.395
  961.8 13.6 fusion.23
  988.9 15.0 fusion.19
  1016.1 28.3 %add_add_fusion.1 = f32[3200,800]{1,0:T(8,128)} fusion(f32[3200,800]{1,0:T(8,128)} %fusion.19, f32[3200,800]{1,0:T(8,128)} %fusion.23, f32[3200,800]{1,0:T(8,128)} %fusion.27, f32[3200,800]{1,0:T(8,128)} %fusion.31, f32[3200,800]{1,0:T(8,128)} %fusion.35, f32[3200,800]{1,0:T(8,128)S(1)} %bitcast.1892, f32[3200,800]{1,0:T(8,128)} %fusion.39, ...), kind=kOutput, calls=%fused_computation.1 | convolution fusion | flops 2967347200 | bytes 83468800 | tf_op jit(solution)/shard_map/bdp,bcp->dc/dot_general | solution.py:65
  1045.4 13.5 fusion.47
  1058.9 17.4 fusion.57
  1076.4 17.5 fusion.67
  1093.8 17.9 %fusion.77 = f32[800,3200]{0,1:T(8,128)} fusion(f32[1,96,3200]{2,1,0:T(8,128)S(1)} %copy-done.225, f32[1,96,800]{2,1,0:T(8,128)S(1)} %copy-done.186), kind=kOutput, calls=%fused_computation.128 | convolution fusion | flops 2968780800 | bytes 11776000 | tf_op jit(solution)/shard_map/bdp,bcp->dc/dot_general | solution.py:65
  1111.8 17.4 fusion.87
  1129.2 17.4 fusion.97
  1146.6 17.6 %fusion.107 = f32[800,3200]{0,1:T(8,128)} fusion(f32[1,96,3200]{2,1,0:T(8,128)S(1)} %copy-done.216, f32[1,96,800]{2,1,0:T(8,128)S(1)} %copy-done.193), kind=kOutput, calls=%fused_computation.176 | convolution fusion | flops 2968780800 | bytes 11776000 | tf_op jit(solution)/shard_map/bdp,bcp->dc/dot_general | solution.py:65
  1164.2 29.4 %add_add_fusion = f32[800,3200]{0,1:T(8,128)} fusion(f32[800,3200]{0,1:T(8,128)} %fusion.107, f32[800,3200]{0,1:T(8,128)} %fusion.97, f32[800,3200]{0,1:T(8,128)} %fusion.87, f32[800,3200]{0,1:T(8,128)} %fusion.77, f32[800,3200]{0,1:T(8,128)} %fusion.67, f32[800,3200]{0,1:T(8,128)S(1)} %fusion.47, f32[800,3200]{0,1:T(8,128)} %fusion.57, ...), kind=kOutput, calls=%fused_computation | convolution fusion | flops 2986700800 | bytes 83456000 | tf_op jit(solution)/shard_map/bdp,bcp->dc/dot_general | solution.py:65
  1227.0 16.6 fusion.287
  1434.4 11.5 all-reduce.394
  1454.5 105.7 %add_add_fusion.2 = f32[800,7,7]{0,2,1:T(8,128)} fusion(f32[800,1,1]{0,2,1:T(1,128)S(1)} %broadcast_in_dim.2494, f32[800,1,1]{0,2,1:T(1,128)S(1)} %broadcast_in_dim.2493, f32[800,1,1]{0,2,1:T(1,128)S(1)} %broadcast_in_dim.2492, f32[800,1,1]{0,2,1:T(1,128)S(1)} %broadcast_in_dim.2491, f32[800,1,1]{0,2,1:T(1,128)S(1)} %broadcast_in_dim.2490, ...), kind=kLoop, calls=%fused_computation.1873 | loop fusion | flops 13720000 | bytes 1587200 | tf_op jit(solution)/shard_map/add | solution.py:138
  1591.5 42.2 %all-reduce.392 = (f32[800]{0:T(1024)}, f32[800]{0:T(1024)}, f32[800]{0:T(1024)}, f32[3200]{0:T(1024)}, f32[800]{0:T(1024)}, /*index=5*/f32[77]{0:T(128)}) all-reduce(f32[800]{0:T(1024)S(1)} %add_add_fusion.8, f32[800]{0:T(1024)S(1)} %add_add_fusion.7, ...), channel_id=1, replica_groups=mesh['step'=8,'rows'=4] {'step','rows'}, use_global_device_ids=true, to_apply=%region_75.76 | all-reduce | flops 6477 | bytes 51816 | tf_op jit(solution)/shard_map/psum | solution.py:253
  1637.0 101.1 %all-reduce.412.cloned.1.call-done = (f32[800,158]{0,1:T(8,128)}, f32[800,7,7]{0,2,1:T(8,128)}, f32[77,800]{1,0:T(8,128)}) async-done(((f32[800,158]{0,1:T(8,128)}, f32[800,7,7]{0,2,1:T(8,128)}, f32[77,800]{1,0:T(8,128)}), (f32[800,158]{0,1:T(8,128)}, f32[800,7,7]{0,2,1:T(8,128)}, f32[77,800]{1,0:T(8,128)})) %all-reduce.412.cloned.1.call-update) | async-done | bytes 908816 | tf_op jit(solution)/shard_map/psum | solution.py:253
  (2054 shorter events, 1012.4 us)
Async XLA Ops:
  8.0 1558.9 %reduce-scatter.9.cloned.1.call-start = ((), (), s32[]{:S(2)}) async-start(), calls=%async_computation.4 | async-start | bytes 12902400 | tf_op jit(solution)/shard_map/reduce_scatter | solution.py:268
  9.2 67.4 %collective-permute-start.2 = (f32[1,77,96]{2,1,0:T(8,128)S(1)}, f32[1,77,96]{2,1,0:T(8,128)S(1)}, u32[]{:S(2)}, u32[]{:S(2)}) collective-permute-start(f32[1,77,96]{2,1,0:T(8,128)S(1)} %bitcast.1912), channel_id=1, source_target_pairs={{0,4},{4,8},{8,12},{12,16},{16,20},{20,24},{24,28},{28,0},{1,5},{5... | collective-permute-start | bytes 88712 | tf_op jit(solution)/shard_map/ppermute | solution.py:32
  11.6 13.0 collective-permute-start.1
  16.1 12.6 collective-permute-start
  85.3 55.9 %collective-permute-start.6 = (f32[1,77,96]{2,1,0:T(8,128)S(1)}, f32[1,77,96]{2,1,0:T(8,128)S(1)}, u32[]{:S(2)}, u32[]{:S(2)}) collective-permute-start(f32[1,77,96]{2,1,0:T(8,128)S(1)} %collective-permute-done.3), channel_id=1, source_target_pairs={{0,4},{4,8},{8,12},{12,16},{16,20},{20,24},{24,28},{28,0},{1,5},{5... | collective-permute-start | bytes 88712 | tf_op jit(solution)/shard_map/ppermute | solution.py:32
  150.9 55.9 %collective-permute-start.10 = (f32[1,77,96]{2,1,0:T(8,128)S(1)}, f32[1,77,96]{2,1,0:T(8,128)S(1)}, u32[]{:S(2)}, u32[]{:S(2)}) collective-permute-start(f32[1,77,96]{2,1,0:T(8,128)S(1)} %collective-permute-done.7), channel_id=1, source_target_pairs={{0,4},{4,8},{8,12},{12,16},{16,20},{20,24},{24,28},{28,0},{1,5},{5... | collective-permute-start | bytes 88712 | tf_op jit(solution)/shard_map/ppermute | solution.py:32
  216.6 54.8 %collective-permute-start.14 = (f32[1,77,96]{2,1,0:T(8,128)S(1)}, f32[1,77,96]{2,1,0:T(8,128)S(1)}, u32[]{:S(2)}, u32[]{:S(2)}) collective-permute-start(f32[1,77,96]{2,1,0:T(8,128)S(1)} %collective-permute-done.11), channel_id=1, source_target_pairs={{0,4},{4,8},{8,12},{12,16},{16,20},{20,24},{24,28},{28,0},{1,5},{5... | collective-permute-start | bytes 88712 | tf_op jit(solution)/shard_map/ppermute | solution.py:32
  281.0 54.7 %collective-permute-start.18 = (f32[1,77,96]{2,1,0:T(8,128)S(1)}, f32[1,77,96]{2,1,0:T(8,128)S(1)}, u32[]{:S(2)}, u32[]{:S(2)}) collective-permute-start(f32[1,77,96]{2,1,0:T(8,128)S(1)} %collective-permute-done.15), channel_id=1, source_target_pairs={{0,4},{4,8},{8,12},{12,16},{16,20},{20,24},{24,28},{28,0},{1,5},{5... | collective-permute-start | bytes 88712 | tf_op jit(solution)/shard_map/ppermute | solution.py:32
  345.5 55.4 %collective-permute-start.22 = (f32[1,77,96]{2,1,0:T(8,128)S(1)}, f32[1,77,96]{2,1,0:T(8,128)S(1)}, u32[]{:S(2)}, u32[]{:S(2)}) collective-permute-start(f32[1,77,96]{2,1,0:T(8,128)S(1)} %collective-permute-done.19), channel_id=1, source_target_pairs={{0,4},{4,8},{8,12},{12,16},{16,20},{20,24},{24,28},{28,0},{1,5},{5... | collective-permute-start | bytes 88712 | tf_op jit(solution)/shard_map/ppermute | solution.py:32
  410.6 56.7 %collective-permute-start.26 = (f32[1,77,96]{2,1,0:T(8,128)S(1)}, f32[1,77,96]{2,1,0:T(8,128)S(1)}, u32[]{:S(2)}, u32[]{:S(2)}) collective-permute-start(f32[1,77,96]{2,1,0:T(8,128)S(1)} %collective-permute-done.23), channel_id=1, source_target_pairs={{0,4},{4,8},{8,12},{12,16},{16,20},{20,24},{24,28},{28,0},{1,5},{5... | collective-permute-start | bytes 88712 | tf_op jit(solution)/shard_map/ppermute | solution.py:32
  617.5 20.8 %collective-permute-start.35 = (f32[1,77,96]{2,1,0:T(8,128)S(1)}, f32[1,77,96]{2,1,0:T(8,128)S(1)}, u32[]{:S(2)}, u32[]{:S(2)}) collective-permute-start(f32[1,77,96]{2,1,0:T(8,128)S(1)} %get-tuple-element.916), channel_id=1, source_target_pairs={{0,28},{4,0},{8,4},{12,8},{16,12},{20,16},{24,20},{28,24},{1,29},{... | collective-permute-start | bytes 88712 | tf_op jit(solution)/shard_map/ppermute | solution.py:32
  676.9 21.0 %collective-permute-start.39 = (f32[1,77,96]{2,1,0:T(8,128)S(1)}, f32[1,77,96]{2,1,0:T(8,128)S(1)}, u32[]{:S(2)}, u32[]{:S(2)}) collective-permute-start(f32[1,77,96]{2,1,0:T(8,128)S(1)} %get-tuple-element.913), channel_id=1, source_target_pairs={{0,28},{4,0},{8,4},{12,8},{16,12},{20,16},{24,20},{28,24},{1,29},{... | collective-permute-start | bytes 88712 | tf_op jit(solution)/shard_map/ppermute | solution.py:32
  735.4 11.2 collective-permute-start.41
  736.7 20.5 %collective-permute-start.43 = (f32[1,77,96]{2,1,0:T(8,128)S(1)}, f32[1,77,96]{2,1,0:T(8,128)S(1)}, u32[]{:S(2)}, u32[]{:S(2)}) collective-permute-start(f32[1,77,96]{2,1,0:T(8,128)S(1)} %get-tuple-element.912), channel_id=1, source_target_pairs={{0,28},{4,0},{8,4},{12,8},{16,12},{20,16},{24,20},{28,24},{1,29},{... | collective-permute-start | bytes 88712 | tf_op jit(solution)/shard_map/ppermute | solution.py:32
  757.4 13.8 collective-permute-start.44
  803.5 18.0 %collective-permute-start.46 = (f32[1,800,96]{1,2,0:T(8,128)S(1)}, f32[1,800,96]{1,2,0:T(8,128)S(1)}, u32[]{:S(2)}, u32[]{:S(2)}) collective-permute-start(f32[1,800,96]{1,2,0:T(8,128)S(1)} %get-tuple-element.753), channel_id=1, source_target_pairs={{0,1},{1,2},{2,3},{4,5},{5,6},{6,7},{8,9},{9,10},{10,11},{12,13},{... | collective-permute-start | bytes 921608 | tf_op jit(solution)/shard_map/ppermute | solution.py:21
  807.1 14.5 collective-permute-start.45
  832.3 15.1 collective-permute-start.48
  882.6 15.8 collective-permute-start.50
  884.0 14.5 collective-permute-start.49
  898.2 10.9 collective-permute-start.51
  909.2 14.5 collective-permute-start.52
  959.2 16.5 collective-permute-start.54
  960.5 15.2 collective-permute-start.53
  975.4 10.9 collective-permute-start.55
  987.0 17.0 collective-permute-start.56
  1044.4 536.2 %reduce-scatter.11.cloned.1.call-start = ((), (), s32[]{:S(2)}) async-start(), calls=%async_computation.5 | async-start | bytes 12902400 | tf_op jit(solution)/shard_map/reduce_scatter | solution.py:269
  1193.7 441.3 %reduce-scatter.13.cloned.1.call-start = ((), (), s32[]{:S(2)}) async-start(), calls=%async_computation.6 | async-start | bytes 2048000
  1447.1 116.1 %collective-permute-start.58 = (f32[1,800,96]{1,2,0:T(8,128)S(1)}, f32[1,800,96]{1,2,0:T(8,128)S(1)}, u32[]{:S(2)}, u32[]{:S(2)}) collective-permute-start(f32[1,800,96]{1,2,0:T(8,128)S(1)} %get-tuple-element.756), channel_id=1, source_target_pairs={{0,1},{1,2},{2,3},{4,5},{5,6},{6,7},{8,9},{9,10},{10,11},{12,13},{... | collective-permute-start | bytes 921608 | tf_op jit(solution)/shard_map/ppermute | solution.py:21
  1448.4 114.8 %collective-permute-start.57 = (f32[1,800,96]{1,2,0:T(8,128)S(1)}, f32[1,800,96]{1,2,0:T(8,128)S(1)}, u32[]{:S(2)}, u32[]{:S(2)}) collective-permute-start(f32[1,800,96]{1,2,0:T(8,128)S(1)} %get-tuple-element.756), channel_id=1, source_target_pairs={{1,0},{2,1},{3,2},{5,4},{6,5},{7,6},{9,8},{10,9},{11,10},{13,12},{... | collective-permute-start | bytes 921608 | tf_op jit(solution)/shard_map/ppermute | solution.py:23
  1570.0 168.0 %all-reduce.412.cloned.1.call-start = ((), (), s32[]{:S(2)}) async-start(), calls=%async_computation.8 | async-start | bytes 2121728 | tf_op jit(solution)/shard_map/psum | solution.py:253
  1580.6 157.5 %reduce-scatter.15.cloned.1.call-start = ((), (), s32[]{:S(2)}) async-start(), calls=%async_computation.7 | async-start | bytes 2048000
  (559 other events, 7228.0 us)
Sparse Core Ops, SparseCore 0:
  1044.6 85.5 reduce-scatter.8
  1193.9 85.3 reduce-scatter.10
  1570.2 37.0 reduce-scatter.12
  1610.0 36.3 reduce-scatter.14
Sparse Core Ops, SparseCore 1:
  1580.6 157.4 all-reduce.411
where the time goes:
time: 1760 us; the launch traced here: 1750 us
  matrix products  694 us (39%)
  other arithmetic  298 us (17%)
  waiting for transfers between devices  231 us (13%)
  local copies, waits for them, and re-layouts  224 us (13%)
  blocking collectives  194 us (11%)
  starting transfers between devices  81 us (5%)
  between operations  26.5 us (2%)
    dot_general x32, matrix products, outer_sum(): jnp.einsum('bdp,bcp->dc', first_factor, second_factor, precision=HIGHEST)  289 us
    dot_general x32, matrix products, contract(): return jnp.einsum('dc,bcp->bdp', weights, values, precision=HIGHEST)  224 us
    dot_general x32, matrix products, transposed(): return jnp.einsum('dc,bdp->bcp', weights, values, precision=HIGHEST)  181 us
    broadcast_in_dim x392, local copies, waits for them, and re-layouts, depthwise(): accumulated = accumulated + kernel[:, tap_row, tap_col, None] * piece  178 us
    add x1, other arithmetic, backward_tick(): grad_w_dw = grad_w_dw + kernel_back(grad_mixed)[0]  106 us
    psum x1, waiting for transfers between devices, per_device(): lax.psum((grad_w_in, grad_b_in, grad_w_dw, grad_bn_gain, grad_bn_bias, gr...  101 us
    select_n x109, other arithmetic, depthwise(): shifted = jnp.where(inside, shifted, jnp.zeros_like(shifted))  89.6 us
    psum x8, blocking collectives, backward_tick(): total_bias, total_gain = lax.psum((local_bias, local_gain), 'rows')  79.3 us
  transfers between devices with their start and end apart: 65, of which 34 were waited for; matrix products, arithmetic and copies ran while one was open for 54% of the time, Pallas kernels for 0%

commit v1 on v0

--- a/solution.py
+++ b/solution.py
@@ -250,20 +250,19 @@
         grad_w_out,
         grad_b_out,
     ) = grad_list
-    small_totals = lax.psum(
-        (
-            grad_w_in,
-            grad_b_in,
-            grad_w_dw,
-            grad_bn_gain,
-            grad_bn_bias,
-            grad_b_up,
-            grad_b_down,
-            grad_w_out,
-            grad_b_out,
-        ),
-        ("step", "rows"),
-    )
+    small_totals = (
+        grad_w_in,
+        grad_b_in,
+        grad_w_dw,
+        grad_bn_gain,
+        grad_bn_bias,
+        grad_b_up,
+        grad_b_down,
+        grad_w_out,
+        grad_b_out,
+    )
+    for mesh_axis in ("rows", "step"):
+        small_totals = lax.psum(small_totals, mesh_axis)
     shares = (
         lax.psum_scatter(grad_w_up, "step", scatter_dimension=0, tiled=True),
         lax.psum_scatter(grad_w_down, "step", scatter_dimension=1, tiled=True),

time: 1760 us -> 1820 us (1.034)
  waiting for transfers between devices: 231 us -> 263 us
  local copies, waits for them, and re-layouts: 224 us -> 247 us
    reduce_scatter x1, waiting for transfers between devices: 0.02 us -> 65.3 us  [per_device(): lax.psum_scatter(grad_w_down, 'step', scatter_dimension=1, tiled=True)]
    psum x1 -> x2, waiting for transfers between devices: 101 us -> 58.3 us  [per_device(): small_totals = lax.psum(small_totals, mesh_axis)]
    unnamed x7 -> x8, waiting for transfers between devices: 0.09 us -> 38.8 us
    broadcast_in_dim x392, local copies, waits for them, and re-layouts: 178 us -> 200 us  [depthwise(): accumulated = accumulated + kernel[:, tap_row, tap_col, None] * piece]
    psum x1 -> x2, blocking collectives: 42.2 us -> 45 us  [per_device(): small_totals = lax.psum(small_totals, mesh_axis)]
  transfers between devices with their start and end apart: 65 -> 66, of which waited for: 34 -> 31; matrix products, arithmetic and copies ran while one was open for 54% -> 53% of each run, Pallas kernels for 0% -> 0%
where the time goes in v1:
time: 1820 us; the launch traced here: 1810 us
  matrix products  693 us (38%)
  other arithmetic  291 us (16%)
  waiting for transfers between devices  263 us (14%)
  local copies, waits for them, and re-layouts  247 us (14%)
  blocking collectives  208 us (11%)
  starting transfers between devices  77.5 us (4%)
  between operations  26.5 us (1%)
    dot_general x32, matrix products, outer_sum(): jnp.einsum('bdp,bcp->dc', first_factor, second_factor, precision=HIGHEST)  296 us
    dot_general x32, matrix products, contract(): return jnp.einsum('dc,bcp->bdp', weights, values, precision=HIGHEST)  220 us
    broadcast_in_dim x392, local copies, waits for them, and re-layouts, depthwise(): accumulated = accumulated + kernel[:, tap_row, tap_col, None] * piece  200 us
    dot_general x32, matrix products, transposed(): return jnp.einsum('dc,bdp->bcp', weights, values, precision=HIGHEST)  177 us
    add x1, other arithmetic, backward_tick(): grad_w_dw = grad_w_dw + kernel_back(grad_mixed)[0]  105 us
    psum x8, blocking collectives, backward_tick(): total_bias, total_gain = lax.psum((local_bias, local_gain), 'rows')  89.5 us
    select_n x109, other arithmetic, depthwise(): shifted = jnp.where(inside, shifted, jnp.zeros_like(shifted))  89.4 us
    psum x8, blocking collectives, per_device(): lax.psum((first_sum, second_sum, local_count), 'rows')  73.6 us
  transfers between devices with their start and end apart: 66, of which 31 were waited for; matrix products, arithmetic and copies ran while one was open for 53% of the time, Pallas kernels for 0%

profile of v1, /device:TPU:0, one launch (start us, length us, event | category | flops | bytes accessed | tf_op | source)
XLA Modules:
  0.0 1805.5 jit_solution(15351352176004870192)
XLA Ops:
  58.0 16.4 fusion.392
  121.5 16.4 fusion.377
  185.5 16.4 fusion.362
  249.9 16.4 fusion.347
  313.1 16.4 fusion.332
  376.6 16.4 fusion.317
  444.0 16.4 fusion.302
  512.4 17.1 fusion.287
  567.9 12.9 fusion.43
  580.8 17.4 fusion.47
  682.9 12.9 fusion.39
  695.9 17.4 fusion.57
  932.8 12.9 fusion.35
  965.6 12.5 fusion.1173
  1007.3 13.2 fusion.31
  1032.2 14.9 fusion.27
  1085.5 13.7 fusion.23
  1112.0 15.0 fusion.19
  1138.4 28.2 %add_add_fusion.1 = f32[3200,800]{1,0:T(8,128)} fusion(f32[3200,800]{1,0:T(8,128)} %fusion.19, f32[3200,800]{1,0:T(8,128)} %fusion.23, f32[3200,800]{1,0:T(8,128)} %fusion.27, f32[3200,800]{1,0:T(8,128)} %fusion.31, f32[3200,800]{1,0:T(8,128)} %fusion.35, f32[3200,800]{1,0:T(8,128)S(1)} %bitcast.1892, f32[3200,800]{1,0:T(8,128)} %fusion.39, ...), kind=kOutput, calls=%fused_computation.1 | convolution fusion | flops 2967347200 | bytes 83468800 | tf_op jit(solution)/shard_map/bdp,bcp->dc/dot_general | solution.py:65
  1167.6 18.8 %fusion.67 = f32[800,3200]{0,1:T(8,128)} fusion(f32[1,96,3200]{2,1,0:T(8,128)} %copy-done.214, f32[1,96,800]{2,1,0:T(8,128)S(1)} %copy-done.165), kind=kOutput, calls=%fused_computation.112 | convolution fusion | flops 2968780800 | bytes 11776000 | tf_op jit(solution)/shard_map/bdp,bcp->dc/dot_general | solution.py:65
  1220.3 17.4 fusion.77
  1271.6 17.6 fusion.87
  1323.1 17.4 fusion.97
  1372.4 17.9 fusion.107
  1421.2 105.0 %add_add_fusion.2 = f32[800,7,7]{0,2,1:T(8,128)} fusion(f32[800,1,1]{0,2,1:T(1,128)S(1)} %broadcast_in_dim.2494, f32[800,1,1]{0,2,1:T(1,128)S(1)} %broadcast_in_dim.2493, f32[800,1,1]{0,2,1:T(1,128)S(1)} %broadcast_in_dim.2492, f32[800,1,1]{0,2,1:T(1,128)S(1)} %broadcast_in_dim.2491, f32[800,1,1]{0,2,1:T(1,128)S(1)} %broadcast_in_dim.2490, ...), kind=kLoop, calls=%fused_computation.1873 | loop fusion | flops 13720000 | bytes 1587200 | tf_op jit(solution)/shard_map/add | solution.py:138
  1538.1 32.4 %add_add_fusion = f32[800,3200]{0,1:T(8,128)} fusion(f32[800,3200]{0,1:T(8,128)} %fusion.107, f32[800,3200]{0,1:T(8,128)} %fusion.97, f32[800,3200]{0,1:T(8,128)} %fusion.87, f32[800,3200]{0,1:T(8,128)} %fusion.77, f32[800,3200]{0,1:T(8,128)} %fusion.67, f32[800,3200]{0,1:T(8,128)} %fusion.47, f32[800,3200]{0,1:T(8,128)} %fusion.57, ...), kind=kOutput, calls=%fused_computation | convolution fusion | flops 2986700800 | bytes 83456000 | tf_op jit(solution)/shard_map/bdp,bcp->dc/dot_general | solution.py:65
  1573.7 16.7 all-reduce.417.cloned.1.call-done
  1590.7 65.3 %reduce-scatter.11.cloned.1.call-done = f32[800,400]{0,1:T(8,128)} async-done(((f32[800,3200]{0,1:T(8,128)}), f32[800,400]{0,1:T(8,128)}) %reduce-scatter.11.cloned.1.call-update) | async-done | bytes 1280016 | tf_op jit(solution)/shard_map/reduce_scatter | solution.py:268
  1666.4 21.7 %all-reduce.394 = (f32[800]{0:T(1024)S(1)}, f32[800]{0:T(1024)S(1)}, f32[800]{0:T(1024)S(1)}, f32[3200]{0:T(1024)S(1)}, f32[800]{0:T(1024)S(1)}, /*index=5*/f32[77]{0:T(128)S(1)}) all-reduce(f32[800]{0:T(1024)S(1)} %add_add_fusion.8, f32[800]{0:T(1024)S(1)} %add_add_fusion.7, ...), channel_id=1, replica_groups=mesh['step'=8,'rows'=4] {'rows'}, use_global_device_ids=true, to_apply=%region_76.77 | all-reduce | flops 6477 | bytes 51816 | tf_op jit(solution)/shard_map/psum | solution.py:265
  1688.1 23.3 %all-reduce.392 = (f32[800]{0:T(1024)}, f32[800]{0:T(1024)}, f32[800]{0:T(1024)}, f32[3200]{0:T(1024)}, f32[800]{0:T(1024)}, /*index=5*/f32[77]{0:T(128)}) all-reduce(f32[800]{0:T(1024)S(1)} %get-tuple-element.700, f32[800]{0:T(1024)S(1)} %get-tuple-element.701, ...), channel_id=1, replica_groups=mesh['step'=8,'rows'=4] {'step'}, use_global_device_ids=true, to_apply=%region_77.78 | all-reduce | flops 6477 | bytes 51816 | tf_op jit(solution)/shard_map/psum | solution.py:265
  1714.6 41.5 %all-reduce.415.cloned.1.call-done = (f32[800,158]{0,1:T(8,128)}, f32[800,7,7]{0,2,1:T(8,128)}, f32[77,800]{1,0:T(8,128)}) async-done(((f32[800,158]{0,1:T(8,128)}, f32[800,7,7]{0,2,1:T(8,128)}, f32[77,800]{1,0:T(8,128)}), (f32[800,158]{0,1:T(8,128)}, f32[800,7,7]{0,2,1:T(8,128)}, f32[77,800]{1,0:T(8,128)})) %all-reduce.415.cloned.1.call-update) | async-done | bytes 908816 | tf_op jit(solution)/shard_map/psum | solution.py:265
  1756.2 38.7 %reduce-scatter.15.cloned.1.call-done = f32[200,400]{1,0:T(8,128)} async-done(((f32[800,400]{1,0:T(8,128)}), f32[200,400]{1,0:T(8,128)}) %reduce-scatter.15.cloned.1.call-update) | async-done | bytes 320016
  (2156 shorter events, 1042.4 us)
Async XLA Ops:
  8.0 1562.5 %reduce-scatter.9.cloned.1.call-start = ((), (), s32[]{:S(2)}) async-start(), calls=%async_computation.4 | async-start | bytes 12902400 | tf_op jit(solution)/shard_map/reduce_scatter | solution.py:267
  9.2 66.0 %collective-permute-start.2 = (f32[1,77,96]{2,1,0:T(8,128)S(1)}, f32[1,77,96]{2,1,0:T(8,128)S(1)}, u32[]{:S(2)}, u32[]{:S(2)}) collective-permute-start(f32[1,77,96]{2,1,0:T(8,128)S(1)} %bitcast.1912), channel_id=1, source_target_pairs={{0,4},{4,8},{8,12},{12,16},{16,20},{20,24},{24,28},{28,0},{1,5},{5... | collective-permute-start | bytes 88712 | tf_op jit(solution)/shard_map/ppermute | solution.py:32
  83.9 54.9 %collective-permute-start.6 = (f32[1,77,96]{2,1,0:T(8,128)S(1)}, f32[1,77,96]{2,1,0:T(8,128)S(1)}, u32[]{:S(2)}, u32[]{:S(2)}) collective-permute-start(f32[1,77,96]{2,1,0:T(8,128)S(1)} %collective-permute-done.3), channel_id=1, source_target_pairs={{0,4},{4,8},{8,12},{12,16},{16,20},{20,24},{24,28},{28,0},{1,5},{5... | collective-permute-start | bytes 88712 | tf_op jit(solution)/shard_map/ppermute | solution.py:32
  148.6 54.1 %collective-permute-start.10 = (f32[1,77,96]{2,1,0:T(8,128)S(1)}, f32[1,77,96]{2,1,0:T(8,128)S(1)}, u32[]{:S(2)}, u32[]{:S(2)}) collective-permute-start(f32[1,77,96]{2,1,0:T(8,128)S(1)} %collective-permute-done.7), channel_id=1, source_target_pairs={{0,4},{4,8},{8,12},{12,16},{16,20},{20,24},{24,28},{28,0},{1,5},{5... | collective-permute-start | bytes 88712 | tf_op jit(solution)/shard_map/ppermute | solution.py:32
  212.4 54.6 %collective-permute-start.14 = (f32[1,77,96]{2,1,0:T(8,128)S(1)}, f32[1,77,96]{2,1,0:T(8,128)S(1)}, u32[]{:S(2)}, u32[]{:S(2)}) collective-permute-start(f32[1,77,96]{2,1,0:T(8,128)S(1)} %collective-permute-done.11), channel_id=1, source_target_pairs={{0,4},{4,8},{8,12},{12,16},{16,20},{20,24},{24,28},{28,0},{1,5},{5... | collective-permute-start | bytes 88712 | tf_op jit(solution)/shard_map/ppermute | solution.py:32
  276.7 53.7 %collective-permute-start.18 = (f32[1,77,96]{2,1,0:T(8,128)S(1)}, f32[1,77,96]{2,1,0:T(8,128)S(1)}, u32[]{:S(2)}, u32[]{:S(2)}) collective-permute-start(f32[1,77,96]{2,1,0:T(8,128)S(1)} %collective-permute-done.15), channel_id=1, source_target_pairs={{0,4},{4,8},{8,12},{12,16},{16,20},{20,24},{24,28},{28,0},{1,5},{5... | collective-permute-start | bytes 88712 | tf_op jit(solution)/shard_map/ppermute | solution.py:32
  340.2 53.6 %collective-permute-start.22 = (f32[1,77,96]{2,1,0:T(8,128)S(1)}, f32[1,77,96]{2,1,0:T(8,128)S(1)}, u32[]{:S(2)}, u32[]{:S(2)}) collective-permute-start(f32[1,77,96]{2,1,0:T(8,128)S(1)} %collective-permute-done.19), channel_id=1, source_target_pairs={{0,4},{4,8},{8,12},{12,16},{16,20},{20,24},{24,28},{28,0},{1,5},{5... | collective-permute-start | bytes 88712 | tf_op jit(solution)/shard_map/ppermute | solution.py:32
  404.4 57.3 %collective-permute-start.26 = (f32[1,77,96]{2,1,0:T(8,128)}, f32[1,77,96]{2,1,0:T(8,128)S(1)}, u32[]{:S(2)}, u32[]{:S(2)}) collective-permute-start(f32[1,77,96]{2,1,0:T(8,128)} %collective-permute-done.23), channel_id=1, source_target_pairs={{0,4},{4,8},{8,12},{12,16},{16,20},{20,24},{24,28},{28,0},{1,5},{5... | collective-permute-start | bytes 88712 | tf_op jit(solution)/shard_map/ppermute | solution.py:32
  564.2 36.1 %collective-permute-start.31 = (f32[1,800,96]{1,2,0:T(8,128)S(1)}, f32[1,800,96]{1,2,0:T(8,128)S(1)}, u32[]{:S(2)}, u32[]{:S(2)}) collective-permute-start(f32[1,800,96]{1,2,0:T(8,128)S(1)} %get-tuple-element.759), channel_id=1, source_target_pairs={{0,1},{1,2},{2,3},{4,5},{5,6},{6,7},{8,9},{9,10},{10,11},{12,13},{... | collective-permute-start | bytes 921608 | tf_op jit(solution)/shard_map/ppermute | solution.py:21
  566.5 33.8 %collective-permute-start.30 = (f32[1,800,96]{1,2,0:T(8,128)S(1)}, f32[1,800,96]{1,2,0:T(8,128)S(1)}, u32[]{:S(2)}, u32[]{:S(2)}) collective-permute-start(f32[1,800,96]{1,2,0:T(8,128)S(1)} %get-tuple-element.759), channel_id=1, source_target_pairs={{1,0},{2,1},{3,2},{5,4},{6,5},{7,6},{9,8},{10,9},{11,10},{13,12},{... | collective-permute-start | bytes 921608 | tf_op jit(solution)/shard_map/ppermute | solution.py:23
  611.2 31.8 %collective-permute-start.32 = (f32[1,77,96]{2,1,0:T(8,128)S(1)}, f32[1,77,96]{2,1,0:T(8,128)S(1)}, u32[]{:S(2)}, u32[]{:S(2)}) collective-permute-start(f32[1,77,96]{2,1,0:T(8,128)S(1)} %get-tuple-element.924), channel_id=1, source_target_pairs={{0,28},{4,0},{8,4},{12,8},{16,12},{20,16},{24,20},{28,24},{1,29},{... | collective-permute-start | bytes 88712 | tf_op jit(solution)/shard_map/ppermute | solution.py:32
  640.8 84.9 %collective-permute-start.35 = (f32[1,77,96]{2,1,0:T(8,128)}, f32[1,77,96]{2,1,0:T(8,128)}, u32[]{:S(2)}, u32[]{:S(2)}) collective-permute-start(f32[1,77,96]{2,1,0:T(8,128)} %get-tuple-element.925), channel_id=1, source_target_pairs={{0,28},{4,0},{8,4},{12,8},{16,12},{20,16},{24,20},{28,24},{1,29},{... | collective-permute-start | bytes 88712 | tf_op jit(solution)/shard_map/ppermute | solution.py:32
  680.2 35.3 %collective-permute-start.34 = (f32[1,800,96]{1,2,0:T(8,128)S(1)}, f32[1,800,96]{1,2,0:T(8,128)S(1)}, u32[]{:S(2)}, u32[]{:S(2)}) collective-permute-start(f32[1,800,96]{1,2,0:T(8,128)S(1)} %get-tuple-element.760), channel_id=1, source_target_pairs={{0,1},{1,2},{2,3},{4,5},{5,6},{6,7},{8,9},{9,10},{10,11},{12,13},{... | collective-permute-start | bytes 921608 | tf_op jit(solution)/shard_map/ppermute | solution.py:21
  681.6 33.9 %collective-permute-start.33 = (f32[1,800,96]{1,2,0:T(8,128)S(1)}, f32[1,800,96]{1,2,0:T(8,128)S(1)}, u32[]{:S(2)}, u32[]{:S(2)}) collective-permute-start(f32[1,800,96]{1,2,0:T(8,128)S(1)} %get-tuple-element.760), channel_id=1, source_target_pairs={{1,0},{2,1},{3,2},{5,4},{6,5},{7,6},{9,8},{10,9},{11,10},{13,12},{... | collective-permute-start | bytes 921608 | tf_op jit(solution)/shard_map/ppermute | solution.py:23
  763.9 34.3 %collective-permute-start.38 = (f32[1,800,96]{1,2,0:T(8,128)S(1)}, f32[1,800,96]{1,2,0:T(8,128)S(1)}, u32[]{:S(2)}, u32[]{:S(2)}) collective-permute-start(f32[1,800,96]{1,2,0:T(8,128)S(1)} %get-tuple-element.758), channel_id=1, source_target_pairs={{0,1},{1,2},{2,3},{4,5},{5,6},{6,7},{8,9},{9,10},{10,11},{12,13},{... | collective-permute-start | bytes 921608 | tf_op jit(solution)/shard_map/ppermute | solution.py:21
  765.4 32.9 %collective-permute-start.37 = (f32[1,800,96]{1,2,0:T(8,128)S(1)}, f32[1,800,96]{1,2,0:T(8,128)S(1)}, u32[]{:S(2)}, u32[]{:S(2)}) collective-permute-start(f32[1,800,96]{1,2,0:T(8,128)S(1)} %get-tuple-element.758), channel_id=1, source_target_pairs={{1,0},{2,1},{3,2},{5,4},{6,5},{7,6},{9,8},{10,9},{11,10},{13,12},{... | collective-permute-start | bytes 921608 | tf_op jit(solution)/shard_map/ppermute | solution.py:23
  850.7 18.3 %collective-permute-start.43 = (f32[1,77,96]{2,1,0:T(8,128)S(1)}, f32[1,77,96]{2,1,0:T(8,128)S(1)}, u32[]{:S(2)}, u32[]{:S(2)}) collective-permute-start(f32[1,77,96]{2,1,0:T(8,128)S(1)} %copy-done.343), channel_id=1, source_target_pairs={{0,28},{4,0},{8,4},{12,8},{16,12},{20,16},{24,20},{28,24},{1,29},{... | collective-permute-start | bytes 88712 | tf_op jit(solution)/shard_map/ppermute | solution.py:32
  869.7 25.6 %collective-permute-start.44 = (f32[1,77,96]{2,1,0:T(8,128)S(1)}, f32[1,77,96]{2,1,0:T(8,128)S(1)}, u32[]{:S(2)}, u32[]{:S(2)}) collective-permute-start(f32[1,77,96]{2,1,0:T(8,128)S(1)} %get-tuple-element.919), channel_id=1, source_target_pairs={{0,28},{4,0},{8,4},{12,8},{16,12},{20,16},{24,20},{28,24},{1,29},{... | collective-permute-start | bytes 88712 | tf_op jit(solution)/shard_map/ppermute | solution.py:32
  927.9 17.9 collective-permute-start.46
  931.3 14.5 collective-permute-start.45
  1004.7 15.8 collective-permute-start.50
  1031.0 16.1 collective-permute-start.52
  1082.9 16.5 collective-permute-start.54
  1084.2 15.2 collective-permute-start.53
  1110.0 17.0 collective-permute-start.56
  1166.7 423.7 %all-reduce.417.cloned.1.call-start = ((), (), s32[]{:S(2)}) async-start(), calls=%async_computation.9 | async-start | bytes 2121728 | tf_op jit(solution)/shard_map/psum | solution.py:265
  1413.6 114.4 %collective-permute-start.58 = (f32[1,800,96]{1,2,0:T(8,128)S(1)}, f32[1,800,96]{1,2,0:T(8,128)S(1)}, u32[]{:S(2)}, u32[]{:S(2)}) collective-permute-start(f32[1,800,96]{1,2,0:T(8,128)S(1)} %get-tuple-element.765), channel_id=1, source_target_pairs={{0,1},{1,2},{2,3},{4,5},{5,6},{6,7},{8,9},{9,10},{10,11},{12,13},{... | collective-permute-start | bytes 921608 | tf_op jit(solution)/shard_map/ppermute | solution.py:21
  1415.0 112.9 %collective-permute-start.57 = (f32[1,800,96]{1,2,0:T(8,128)S(1)}, f32[1,800,96]{1,2,0:T(8,128)S(1)}, u32[]{:S(2)}, u32[]{:S(2)}) collective-permute-start(f32[1,800,96]{1,2,0:T(8,128)S(1)} %get-tuple-element.765), channel_id=1, source_target_pairs={{1,0},{2,1},{3,2},{5,4},{6,5},{7,6},{9,8},{10,9},{11,10},{13,12},{... | collective-permute-start | bytes 921608 | tf_op jit(solution)/shard_map/ppermute | solution.py:23
  1538.0 118.0 %reduce-scatter.11.cloned.1.call-start = ((), (), s32[]{:S(2)}) async-start(), calls=%async_computation.5 | async-start | bytes 12902400 | tf_op jit(solution)/shard_map/reduce_scatter | solution.py:268
  1570.5 142.2 %reduce-scatter.13.cloned.1.call-start = ((), (), s32[]{:S(2)}) async-start(), calls=%async_computation.6 | async-start | bytes 2048000
  1573.7 182.5 %all-reduce.415.cloned.1.call-start = ((), (), s32[]{:S(2)}) async-start(), calls=%async_computation.8 | async-start | bytes 2121728 | tf_op jit(solution)/shard_map/psum | solution.py:265
  1590.5 204.4 %reduce-scatter.15.cloned.1.call-start = ((), (), s32[]{:S(2)}) async-start(), calls=%async_computation.7 | async-start | bytes 2048000
  (609 other events, 7327.0 us)
Sparse Core Ops, SparseCore 0:
  1166.8 85.3 reduce-scatter.8
  1570.6 85.3 reduce-scatter.10
  1658.3 37.8 reduce-scatter.12
  1700.0 56.1 all-reduce.414
  1759.0 35.8 reduce-scatter.14
Sparse Core Ops, SparseCore 1:
  1538.1 52.3 all-reduce.416
